TPU v7x, 32 devices: a whole 2x2x4 slice. The times are simulated.
32 devices in a mesh: dp: 16 (over z, y, core), tensor: 2 (over x).
Axes of the slice: x: 2, y: 2, z: 4, core: 2. Of those that a mesh axis runs over, the one named last changes fastest.
Arguments:
- block_input: bfloat16 [32768, 1024], P(('dp', 'tensor')), may hold values from -6 to 6
- mixer_gain: float32 [1024], replicated, may hold values from 0.25 to 1.75
- in_weight: bfloat16 [1024, 3, 1024], P(None, None, 'tensor'), may hold values from -0.1875 to 0.1875
- conv_kernel: bfloat16 [3, 1024], P(None, 'tensor'), may hold values from -3.5 to 3.5
- out_weight: bfloat16 [1024, 1024], P('tensor'), may hold values from -0.1875 to 0.1875
- ffn_gain: float32 [1024], replicated, may hold values from 0.25 to 1.75
- gate_weight: bfloat16 [1024, 4608], P(None, 'tensor'), may hold values from -0.1875 to 0.1875
- up_weight: bfloat16 [1024, 4608], P(None, 'tensor'), may hold values from -0.1875 to 0.1875
- down_weight: bfloat16 [4608, 1024], P('tensor'), may hold values from -0.09375 to 0.09375
- output_grad: bfloat16 [32768, 1024], P(('dp', 'tensor')), may hold values from -6 to 6
- lengths: int32 [32], P('dp'), may hold values from 256 to 1024, as said below
Outputs:
- block_output: bfloat16 [32768, 1024], P(('dp', 'tensor'))
- input_grad: bfloat16 [32768, 1024], P(('dp', 'tensor'))
- mixer_gain_grad: float32 [1024], replicated
- in_weight_grad: float32 [1024, 3, 1024], P(None, None, 'tensor')
- conv_kernel_grad: float32 [3, 1024], P(None, 'tensor')
- out_weight_grad: float32 [1024, 1024], P('tensor')
- ffn_gain_grad: float32 [1024], replicated
- gate_weight_grad: float32 [1024, 4608], P(None, 'tensor')
- up_weight_grad: float32 [1024, 4608], P(None, 'tensor')
- down_weight_grad: float32 [4608, 1024], P('tensor')
Inputs may be any that keep to these rules, and one draw needn't show every extreme that they name: `lengths`: each slot holds one sequence at positions 0 to its length - 1; some slot has length 1024 and some 1024 // 4.
All inputs are finite; a program needn't handle non-finite values.
Results may differ from a plain program's by a relative error of at most 0.022.
Values may be sent and summed in bfloat16 or wider, within the bound.
A program may use at most 256 MiB of HBM per device.

v0:
```python
import jax
import jax.numpy as jnp
from jax import lax
from jax.sharding import PartitionSpec as P

KERNEL = 3
eps = 1e-05


def rms_forward(values, gain_values):
    inverse = lax.rsqrt(jnp.mean(values * values, axis=-1, keepdims=True) + eps)
    return (values * inverse * gain_values, inverse)


def rms_backward(values, inverse, gain_values, upstream):
    weighted = upstream * gain_values
    gain_part = jnp.sum(upstream * values * inverse, axis=0)
    through = inverse * weighted - values * inverse**3 * jnp.mean(
        weighted * values, axis=-1, keepdims=True
    )
    return (through, gain_part)


def local(
    block_input,
    mixer_gain,
    in_weight,
    conv_kernel,
    out_weight,
    ffn_gain,
    gate_weight,
    up_weight,
    down_weight,
    output_grad,
    lengths,
):
    local_rows = block_input.shape[0]
    model_width = block_input.shape[1]
    channels = in_weight.shape[2]
    slot_count = lengths.shape[0]
    source = block_input.astype(jnp.float32)
    normed_one, inverse_one = rms_forward(source, mixer_gain)
    gathered_one = lax.all_gather(normed_one.astype(jnp.bfloat16), "tensor", axis=0, tiled=True)
    group_rows = gathered_one.shape[0]
    slot_length = group_rows // slot_count
    in_flat = in_weight.reshape(model_width, 3 * channels)
    projected = jnp.dot(gathered_one, in_flat, preferred_element_type=jnp.float32).reshape(
        group_rows, 3, channels
    )
    b_part = projected[:, 0]
    c_part = projected[:, 1]
    x_part = projected[:, 2]
    mixed = (b_part * x_part).reshape(slot_count, slot_length, channels)
    kernel_values = conv_kernel.astype(jnp.float32)
    padded = jnp.pad(mixed, ((0, 0), (KERNEL - 1, 0), (0, 0)))
    convolved = jnp.zeros_like(mixed)
    for offset in range(KERNEL):
        convolved = convolved + kernel_values[offset] * padded[:, offset : offset + slot_length]
    convolved = convolved.reshape(group_rows, channels)
    gated = (c_part * convolved).astype(jnp.bfloat16)
    hidden = source + lax.psum_scatter(
        jnp.dot(gated, out_weight, preferred_element_type=jnp.float32).astype(jnp.bfloat16),
        "tensor",
        scatter_dimension=0,
        tiled=True,
    ).astype(jnp.float32)
    normed_two, inverse_two = rms_forward(hidden, ffn_gain)
    gathered_two = lax.all_gather(normed_two.astype(jnp.bfloat16), "tensor", axis=0, tiled=True)
    gate_value = jnp.dot(gathered_two, gate_weight, preferred_element_type=jnp.float32)
    up_value = jnp.dot(gathered_two, up_weight, preferred_element_type=jnp.float32)
    sigmoid_gate = jax.nn.sigmoid(gate_value)
    silu_value = gate_value * sigmoid_gate
    inner_low = (silu_value * up_value).astype(jnp.bfloat16)
    block_output = (
        hidden
        + lax.psum_scatter(
            jnp.dot(inner_low, down_weight, preferred_element_type=jnp.float32).astype(
                jnp.bfloat16
            ),
            "tensor",
            scatter_dimension=0,
            tiled=True,
        ).astype(jnp.float32)
    ).astype(jnp.bfloat16)
    row_index = lax.axis_index("tensor") * local_rows + jnp.arange(local_rows, dtype=jnp.int32)
    slot_of = row_index // slot_length
    position = row_index % slot_length
    matched = (slot_of[:, None] == jnp.arange(slot_count, dtype=jnp.int32)[None, :]) & (
        position[:, None] < lengths[None, :]
    )
    token_mask = jnp.any(matched, axis=1).astype(jnp.float32)
    cotangent = output_grad.astype(jnp.float32) * token_mask[:, None]
    grad_rows = lax.all_gather(cotangent.astype(jnp.bfloat16), "tensor", axis=0, tiled=True)
    inner_grad = jnp.einsum("rd,fd->rf", grad_rows, down_weight, preferred_element_type=jnp.float32)
    down_weight_grad = jnp.einsum(
        "rf,rd->fd", inner_low, grad_rows, preferred_element_type=jnp.float32
    )
    gate_grad = (
        inner_grad * up_value * sigmoid_gate * (1.0 + gate_value * (1.0 - sigmoid_gate))
    ).astype(jnp.bfloat16)
    up_grad = (inner_grad * silu_value).astype(jnp.bfloat16)
    gate_weight_grad = jnp.einsum(
        "rd,rf->df", gathered_two, gate_grad, preferred_element_type=jnp.float32
    )
    up_weight_grad = jnp.einsum(
        "rd,rf->df", gathered_two, up_grad, preferred_element_type=jnp.float32
    )
    from_gate = jnp.einsum("rf,df->rd", gate_grad, gate_weight, preferred_element_type=jnp.float32)
    normed_two_grad = lax.psum_scatter(
        (
            from_gate
            + jnp.einsum("rf,df->rd", up_grad, up_weight, preferred_element_type=jnp.float32)
        ).astype(jnp.bfloat16),
        "tensor",
        scatter_dimension=0,
        tiled=True,
    ).astype(jnp.float32)
    through_two, ffn_gain_part = rms_backward(hidden, inverse_two, ffn_gain, normed_two_grad)
    hidden_grad = cotangent + through_two
    hidden_rows = lax.all_gather(hidden_grad.astype(jnp.bfloat16), "tensor", axis=0, tiled=True)
    gated_grad = jnp.einsum(
        "rd,cd->rc", hidden_rows, out_weight, preferred_element_type=jnp.float32
    )
    out_weight_grad = jnp.einsum(
        "rc,rd->cd", gated, hidden_rows, preferred_element_type=jnp.float32
    )
    c_grad = gated_grad * convolved
    conv_grad = (gated_grad * c_part).reshape(slot_count, slot_length, channels)
    padded_after = jnp.pad(conv_grad, ((0, 0), (0, KERNEL - 1), (0, 0)))
    mixed_grad = jnp.zeros_like(conv_grad)
    kernel_rows = []
    for offset in range(KERNEL):
        shift_start = KERNEL - 1 - offset
        mixed_grad = (
            mixed_grad
            + kernel_values[offset] * padded_after[:, shift_start : shift_start + slot_length]
        )
        kernel_rows.append(
            jnp.sum(conv_grad * padded[:, offset : offset + slot_length], axis=(0, 1))
        )
    conv_kernel_grad = jnp.stack(kernel_rows, axis=0)
    mixed_grad = mixed_grad.reshape(group_rows, channels)
    projected_grad = jnp.stack([mixed_grad * x_part, c_grad, mixed_grad * b_part], axis=1).astype(
        jnp.bfloat16
    )
    in_weight_grad = jnp.einsum(
        "rd,rkc->dkc", gathered_one, projected_grad, preferred_element_type=jnp.float32
    )
    normed_one_grad = lax.psum_scatter(
        jnp.einsum(
            "rkc,dkc->rd", projected_grad, in_weight, preferred_element_type=jnp.float32
        ).astype(jnp.bfloat16),
        "tensor",
        scatter_dimension=0,
        tiled=True,
    ).astype(jnp.float32)
    through_one, mixer_gain_part = rms_backward(source, inverse_one, mixer_gain, normed_one_grad)
    input_grad = (hidden_grad + through_one).astype(jnp.bfloat16)
    (
        in_weight_grad,
        conv_kernel_grad,
        out_weight_grad,
        gate_weight_grad,
        up_weight_grad,
        down_weight_grad,
    ) = (
        lax.psum(in_weight_grad.astype(jnp.bfloat16), "dp").astype(jnp.float32),
        lax.psum(conv_kernel_grad.astype(jnp.bfloat16), "dp").astype(jnp.float32),
        lax.psum(out_weight_grad.astype(jnp.bfloat16), "dp").astype(jnp.float32),
        lax.psum(gate_weight_grad.astype(jnp.bfloat16), "dp").astype(jnp.float32),
        lax.psum(up_weight_grad.astype(jnp.bfloat16), "dp").astype(jnp.float32),
        lax.psum(down_weight_grad.astype(jnp.bfloat16), "dp").astype(jnp.float32),
    )
    mixer_gain_grad, ffn_gain_grad = lax.psum((mixer_gain_part, ffn_gain_part), ("dp", "tensor"))
    return (
        block_output,
        input_grad,
        mixer_gain_grad,
        in_weight_grad,
        conv_kernel_grad,
        out_weight_grad,
        ffn_gain_grad,
        gate_weight_grad,
        up_weight_grad,
        down_weight_grad,
    )


def solution(mesh):
    return jax.shard_map(
        local,
        mesh=mesh,
        in_specs=(
            P(("dp", "tensor"), None),
            P(),
            P(None, None, "tensor"),
            P(None, "tensor"),
            P("tensor", None),
            P(),
            P(None, "tensor"),
            P(None, "tensor"),
            P("tensor", None),
            P(("dp", "tensor"), None),
            P("dp"),
        ),
        out_specs=(
            P(("dp", "tensor"), None),
            P(("dp", "tensor"), None),
            P(),
            P(None, None, "tensor"),
            P(None, "tensor"),
            P("tensor", None),
            P(),
            P(None, "tensor"),
            P(None, "tensor"),
            P("tensor", None),
        ),
        check_vma=False,
    )
```

profile of v0, /device:TPU:0, one launch (start us, length us, event | category | flops | bytes accessed | tf_op | source)
XLA Modules:
  0.0 967.7 jit_solution(12564560113143871038)
XLA Ops:
  7.2 2.1 fusion.12
  10.6 3.5 fusion.14
  14.1 4.6 copy.24
  18.8 54.9 %all-gather.5.cloned.1.call-done = bf16[2048,1024]{1,0:T(8,128)(2,1)} async-done(((bf16[1024,1024]{1,0:T(8,128)(2,1)}), bf16[2048,1024]{1,0:T(8,128)(2,1)}) %all-gather.5.cloned.1.call-update) | async-done | bytes 4194320 | tf_op jit(solution)/shard_map/all_gather | solution.py:43
  73.7 9.4 fusion.26
  84.2 1.2 multiply_add_fusion.1
  85.5 2.2 copy-done.3
  87.6 1.3 copy-done.4
  90.9 1.3 copy-done.12
  92.2 4.4 convolution_convert_fusion.4
  96.6 54.4 %reduce-scatter.5.cloned.1.call-done = bf16[1024,1024]{1,0:T(8,128)(2,1)} async-done(((bf16[2048,1024]{1,0:T(8,128)(2,1)}), bf16[1024,1024]{1,0:T(8,128)(2,1)}) %reduce-scatter.5.cloned.1.call-update) | async-done | bytes 2097168 | tf_op jit(solution)/shard_map/reduce_scatter | solution.py:61
  151.0 2.5 multiply_reduce_fusion.2
  154.7 2.1 multiply_convert_fusion.3
  158.1 3.3 fusion.28
  161.5 52.2 %all-gather.7.cloned.1.call-done = bf16[2048,1024]{1,0:T(8,128)(2,1)} async-done(((bf16[1024,1024]{1,0:T(8,128)(2,1)}), bf16[2048,1024]{1,0:T(8,128)(2,1)}) %all-gather.7.cloned.1.call-update) | async-done | bytes 4194320 | tf_op jit(solution)/shard_map/all_gather | solution.py:68
  213.7 16.9 %fusion.46 = f32[2048,2304]{1,0:T(8,128)} fusion(bf16[2048,1024]{1,0:T(8,128)(2,1)} %all-gather.7.cloned.1.call-done, bf16[1024,2304]{1,0:T(8,128)(2,1)} %param.18), kind=kOutput, calls=%fused_computation.96 | convolution fusion | flops 9663676416 | bytes 27787264 | tf_op jit(solution)/shard_map/dot_general | solution.py:70
  230.6 15.3 %fusion.45 = f32[2048,2304]{1,0:T(8,128)} fusion(bf16[2048,1024]{1,0:T(8,128)(2,1)S(1)} %copy-done.37, bf16[1024,2304]{1,0:T(8,128)(2,1)} %param.17), kind=kOutput, calls=%fused_computation.95 | convolution fusion | flops 9663676416 | bytes 27787264 | tf_op jit(solution)/shard_map/dot_general | solution.py:69
  245.9 26.7 %all-gather.9.cloned.1.call-done = bf16[2048,1024]{1,0:T(8,128)(2,1)} async-done(((bf16[1024,1024]{1,0:T(8,128)(2,1)}), bf16[2048,1024]{1,0:T(8,128)(2,1)}) %all-gather.9.cloned.1.call-update) | async-done | bytes 4194320 | tf_op jit(solution)/shard_map/all_gather | solution.py:93
  272.6 35.7 %multiply_convert_fusion = (bf16[2048,2304]{1,0:T(8,128)(2,1)}, bf16[2048,2304]{1,0:T(8,128)(2,1)}, bf16[2048,2304]{1,0:T(8,128)(2,1)}) fusion(f32[2048,2304]{1,0:T(8,128)} %fusion.45, f32[2048,2304]{1,0:T(8,128)} %fusion.46, bf16[2048,1024]{1,0:T(8,128)(2,1)} %all-gather.9.cloned.1.call-done, bf16[2304,1024]{1,0:T(8,128)(2,1)} %param.19), kind=kOutput, calls=%fused_computation | convolution fusion | flops 9734455296 | bytes 74973184 | tf_op jit(solution)/shard_map/rd,fd->rf/dot_general | solution.py:94
  308.2 14.0 %fusion.47 = f32[2048,1024]{1,0:T(8,128)S(1)} fusion(bf16[2048,2304]{1,0:T(8,128)(2,1)} %get-tuple-element.27, bf16[1024,2304]{1,0:T(8,128)(2,1)} %param.17), kind=kOutput, calls=%fused_computation.97 | convolution fusion | flops 9663676416 | bytes 22544384 | tf_op jit(solution)/shard_map/rf,df->rd/dot_general | solution.py:108
  322.3 14.3 %add_convert_fusion = bf16[2048,1024]{1,0:T(8,128)(2,1)} fusion(f32[2048,1024]{1,0:T(8,128)S(1)} %fusion.47, bf16[2048,2304]{1,0:T(8,128)(2,1)S(1)} %copy-done.39, bf16[1024,2304]{1,0:T(8,128)(2,1)} %param.18), kind=kOutput, calls=%fused_computation.12 | convolution fusion | flops 9667870720 | bytes 26738688 | tf_op jit(solution)/shard_map/rf,df->rd/dot_general | solution.py:112
  336.7 15.2 %convolution_convert_fusion.3 = bf16[2048,1024]{1,0:T(8,128)(2,1)} fusion(bf16[2048,2304]{1,0:T(8,128)(2,1)} %get-tuple-element.28, bf16[2304,1024]{1,0:T(8,128)(2,1)} %param.19), kind=kOutput, calls=%fused_computation.66 | convolution fusion | flops 9665773568 | bytes 18350080 | tf_op jit(solution)/shard_map/dot_general | solution.py:77
  352.0 39.1 %reduce-scatter.9.cloned.1.call-done = bf16[1024,1024]{1,0:T(8,128)(2,1)} async-done(((bf16[2048,1024]{1,0:T(8,128)(2,1)}), bf16[1024,1024]{1,0:T(8,128)(2,1)}) %reduce-scatter.9.cloned.1.call-update) | async-done | bytes 2097168 | tf_op jit(solution)/shard_map/reduce_scatter | solution.py:109
  391.1 3.9 fusion.11
  395.0 52.6 %reduce-scatter.7.cloned.1.call-done = bf16[1024,1024]{1,0:T(8,128)(2,1)} async-done(((bf16[2048,1024]{1,0:T(8,128)(2,1)}), bf16[1024,1024]{1,0:T(8,128)(2,1)}) %reduce-scatter.7.cloned.1.call-update) | async-done | bytes 2097168 | tf_op jit(solution)/shard_map/reduce_scatter | solution.py:76
  447.6 6.8 fusion.42
  454.4 56.8 %all-gather.11.cloned.1.call-done = bf16[2048,1024]{1,0:T(8,128)(2,1)} async-done(((bf16[1024,1024]{1,0:T(8,128)(2,1)}), bf16[2048,1024]{1,0:T(8,128)(2,1)}) %all-gather.11.cloned.1.call-update) | async-done | bytes 4194320 | tf_op jit(solution)/shard_map/all_gather | solution.py:120
  511.3 10.4 %multiply_reduce_fusion.1 = (bf16[512]{0:T(512)(128)(2,1)S(1)}, bf16[512]{0:T(512)(128)(2,1)S(1)}, f32[2048,512]{1,0:T(8,128)}, f32[2048,512]{1,0:T(8,128)}) fusion(f32[2,1024,512]{2,1,0:T(8,128)} %bitcast.78, f32[2048,3,512]{2,0,1:T(8,128)} %copy-done.3, bf16[2048,1024]{1,0:T(8,128)(2,1)} %all-gather.11.cloned.1.call-done, bf16[512,1024]{1,0:T(8,128)(2,1)S(1)} %copy-done), kind=kOutput, calls=%fused_computation.54 | convolution fusion | flops 2152725504 | bytes 22022144 | tf_op jit(solution)/shard_map/rd,cd->rc/dot_general | solution.py:121
  521.8 5.0 fusion.23
  526.8 8.4 multiply_add_fusion
  535.2 6.1 fusion.20
  541.3 10.1 %bitcast_convert_fusion = bf16[2048,1024]{1,0:T(8,128)(2,1)} fusion(bf16[1024,3,512]{2,0,1:T(8,128)(2,1)S(1)} %copy-done.10, bf16[2048,1,512]{2,0,1:T(8,128)(2,1)} %get-tuple-element.30, bf16[2048,1,512]{2,0,1:T(8,128)(2,1)} %bitcast.84, bf16[2048,1,512]{2,0,1:T(8,128)(2,1)} %get-tuple-element.29), kind=kOutput, calls=%fused_computation.11 | convolution fusion | flops 6450839552 | bytes 13631488 | tf_op jit(solution)/shard_map/rkc,dkc->rd/dot_general | solution.py:150
  551.5 15.6 %convolution_convert_fusion.2 = bf16[2304,1024]{1,0:T(8,128)(2,1)} fusion(bf16[2048,2304]{1,0:T(8,128)(2,1)} %get-tuple-element.28, bf16[2048,1024]{1,0:T(8,128)(2,1)} %all-gather.9.cloned.1.call-done), kind=kOutput, calls=%fused_computation.16 | convolution fusion | flops 9666035712 | bytes 18350080 | tf_op jit(solution)/shard_map/rf,rd->fd/dot_general | solution.py:95
  567.1 14.1 %convolution_convert_fusion = bf16[1024,2304]{1,0:T(8,128)(2,1)} fusion(bf16[2048,1024]{1,0:T(8,128)(2,1)S(1)} %copy-done.38, bf16[2048,2304]{1,0:T(8,128)(2,1)} %get-tuple-element.26), kind=kOutput, calls=%fused_computation.14 | convolution fusion | flops 9666035712 | bytes 18350080 | tf_op jit(solution)/shard_map/rd,rf->df/dot_general | solution.py:105
  581.2 12.3 %convolution_convert_fusion.1 = bf16[1024,2304]{1,0:T(8,128)(2,1)} fusion(bf16[2048,1024]{1,0:T(8,128)(2,1)S(1)} %copy-done.38, bf16[2048,2304]{1,0:T(8,128)(2,1)S(1)} %bitcast.93), kind=kOutput, calls=%fused_computation.15 | convolution fusion | flops 9666035712 | bytes 18350080 | tf_op jit(solution)/shard_map/rd,rf->df/dot_general | solution.py:102
  593.6 3.3 convolution_convert_fusion.5
  598.2 8.5 fusion.31
  606.7 5.5 fusion.19
  612.2 34.8 %psum.58 = bf16[3,512]{1,0:T(4,128)(2,1)S(1)} all-reduce(bf16[3,512]{1,0:T(4,128)(2,1)S(1)} %pad_maximum_fusion.5), channel_id=1, replica_groups=mesh['dp'=16,'tensor'=2] {'dp'}, use_global_device_ids=true, to_apply=%region_15.16 | all-reduce | flops 1536 | bytes 6144 | tf_op jit(solution)/shard_map/psum | solution.py:168
  647.7 3.3 fusion.18
  650.9 38.5 %all-reduce.2 = (f32[1024]{0:T(1024)}, f32[1024]{0:T(1024)}) all-reduce(f32[1024]{0:T(1024)S(1)} %get-tuple-element.14, f32[1024]{0:T(1024)S(1)} %get-tuple-element.12), channel_id=1, replica_groups=mesh['dp'=16,'tensor'=2] {'dp','tensor'}, use_global_device_ids=true, to_apply=%region_10.11 | all-reduce | flops 2048 | bytes 16384 | tf_op jit(solution)/shard_map/psum | solution.py:174
  689.5 4.5 fusion.6
  694.0 245.0 %all-reduce.6.cloned.1.call-done = (bf16[1024,3,512]{2,0,1:T(8,128)(2,1)}, bf16[512,1024]{1,0:T(8,128)(2,1)}, bf16[1024,2304]{1,0:T(8,128)(2,1)}, bf16[1024,2304]{1,0:T(8,128)(2,1)}, bf16[2304,1024]{1,0:T(8,128)(2,1)}) async-done(((bf16[1024,3,512]{2,0,1:T(8,128)(2,1)}, bf16[512,1024]{1,0:T(8,128)(2,1)}, bf16[1024,2304]{1,0:T(8,128)(2,1)}, bf16[1024,2304]{1,0:T(8,128)(2,1)}, bf16[2304,1024]{1,0:T(8,128)(2,1)}), ...) | async-done | bytes 18350096 | tf_op jit(solution)/shard_map/psum | solution.py:167
  939.0 2.9 convert_element_type.135
  942.0 4.1 convert_element_type.132
  946.1 5.5 convert_element_type.137
  951.6 4.4 convert_element_type.139
  956.0 4.9 convert_element_type.141
  (135 shorter events, 9.2 us)
Async XLA Ops:
  7.2 85.0 %copy-start = (bf16[512,1024]{1,0:T(8,128)(2,1)S(1)}, bf16[512,1024]{1,0:T(8,128)(2,1)}, u32[]{:S(2)}) copy-start(bf16[512,1024]{1,0:T(8,128)(2,1)} %param.15) | copy-start | bytes 3145732
  7.2 66.5 %all-gather.5.cloned.1.call-start = ((), (), s32[]{:S(2)}) async-start(), calls=%async_computation.4 | async-start | bytes 6291456 | tf_op jit(solution)/shard_map/all_gather | solution.py:43
  14.0 4.7 copy-start.34
  14.1 137.0 %reduce-scatter.5.cloned.1.call-start = ((), (), s32[]{:S(2)}) async-start(), calls=%async_computation.5 | async-start | bytes 6291456 | tf_op jit(solution)/shard_map/reduce_scatter | solution.py:61
  18.8 65.4 %copy-start.26 = (f32[1,512]{1,0:T(1,128)}, f32[1,512]{1,0:T(1,128)S(1)}, u32[]{:S(2)}) copy-start(f32[1,512]{1,0:T(1,128)S(1)} %get-tuple-element.36) | copy-start | bytes 6148
  18.8 65.4 %copy-start.28 = (f32[1,512]{1,0:T(1,128)}, f32[1,512]{1,0:T(1,128)S(1)}, u32[]{:S(2)}) copy-start(f32[1,512]{1,0:T(1,128)S(1)} %get-tuple-element.37) | copy-start | bytes 6148
  18.8 65.4 %copy-start.30 = (f32[1,512]{1,0:T(1,128)}, f32[1,512]{1,0:T(1,128)S(1)}, u32[]{:S(2)}) copy-start(f32[1,512]{1,0:T(1,128)S(1)} %get-tuple-element.38) | copy-start | bytes 6148
  83.1 4.5 copy-start.3
  84.2 4.7 copy-start.4
  96.5 54.5 %copy-start.1 = (bf16[1024,1024]{1,0:T(8,128)(2,1)S(1)}, bf16[1024,1024]{1,0:T(8,128)(2,1)}, u32[]{:S(2)}) copy-start(bf16[1024,1024]{1,0:T(8,128)(2,1)} %param.11) | copy-start | bytes 6291460
  96.5 58.2 %copy-start.21 = (f32[1024]{0:T(1024)S(1)}, f32[1024]{0:T(1024)}, u32[]{:S(2)}) copy-start(f32[1024]{0:T(1024)} %param.16) | copy-start | bytes 12292
  96.6 117.2 %all-gather.7.cloned.1.call-start = ((), (), s32[]{:S(2)}) async-start(), calls=%async_computation.6 | async-start | bytes 6291456 | tf_op jit(solution)/shard_map/all_gather | solution.py:68
  156.8 115.7 %all-gather.9.cloned.1.call-start = ((), (), s32[]{:S(2)}) async-start(), calls=%async_computation.8 | async-start | bytes 6291456 | tf_op jit(solution)/shard_map/all_gather | solution.py:93
  161.5 229.6 %reduce-scatter.9.cloned.1.call-start = ((), (), s32[]{:S(2)}) async-start(), calls=%async_computation.9 | async-start | bytes 6291456 | tf_op jit(solution)/shard_map/reduce_scatter | solution.py:109
  213.7 16.9 %copy-start.37 = (bf16[2048,1024]{1,0:T(8,128)(2,1)S(1)}, bf16[2048,1024]{1,0:T(8,128)(2,1)}, u32[]{:S(2)}) copy-start(bf16[2048,1024]{1,0:T(8,128)(2,1)} %all-gather.7.cloned.1.call-done) | copy-start | bytes 12582916
  308.2 14.1 %copy-start.39 = (bf16[2048,2304]{1,0:T(8,128)(2,1)S(1)}, bf16[2048,2304]{1,0:T(8,128)(2,1)}, u32[]{:S(2)}) copy-start(bf16[2048,2304]{1,0:T(8,128)(2,1)} %get-tuple-element.26) | copy-start | bytes 28311556
  336.6 111.0 %reduce-scatter.7.cloned.1.call-start = ((), (), s32[]{:S(2)}) async-start(), calls=%async_computation.7 | async-start | bytes 6291456 | tf_op jit(solution)/shard_map/reduce_scatter | solution.py:76
  351.9 39.2 %copy-start.2 = (bf16[1024,1024]{1,0:T(8,128)(2,1)S(1)}, bf16[1024,1024]{1,0:T(8,128)(2,1)}, u32[]{:S(2)}) copy-start(bf16[1024,1024]{1,0:T(8,128)(2,1)} %param.11) | copy-start | bytes 6291460
  351.9 39.2 %copy-start.20 = (f32[1024]{0:T(1024)S(1)}, f32[1024]{0:T(1024)}, u32[]{:S(2)}) copy-start(f32[1024]{0:T(1024)} %copy-done.19) | copy-start | bytes 12292
  351.9 39.2 %copy-start.22 = (f32[1024]{0:T(1024)S(1)}, f32[1024]{0:T(1024)}, u32[]{:S(2)}) copy-start(f32[1024]{0:T(1024)} %param.16) | copy-start | bytes 12292
  351.9 95.7 %copy-start.25 = (f32[1024]{0:T(1024)S(1)}, f32[1024]{0:T(1024)}, u32[]{:S(2)}) copy-start(f32[1024]{0:T(1024)} %copy-done.24) | copy-start | bytes 12292
  351.9 95.7 %copy-start.33 = (f32[1024]{0:T(1024)S(1)}, f32[1024]{0:T(1024)}, u32[]{:S(2)}) copy-start(f32[1024]{0:T(1024)} %get-tuple-element.34) | copy-start | bytes 12292
  351.9 159.4 %all-gather.11.cloned.1.call-start = ((), (), s32[]{:S(2)}) async-start(), calls=%async_computation.10 | async-start | bytes 6291456 | tf_op jit(solution)/shard_map/all_gather | solution.py:120
  454.4 193.3 %reduce-scatter.11.cloned.1.call-start = ((), (), s32[]{:S(2)}) async-start(), calls=%async_computation.11 | async-start | bytes 6291456 | tf_op jit(solution)/shard_map/reduce_scatter | solution.py:149
  511.3 10.5 %copy-start.6 = (f32[2,1024,512]{2,1,0:T(8,128)S(1)}, f32[2,1024,512]{2,1,0:T(8,128)}, u32[]{:S(2)}) copy-start(f32[2,1024,512]{2,1,0:T(8,128)} %copy-done.5) | copy-start | bytes 12582916
  511.3 23.9 %slice-start = ((s8[12582912]{0:T(1024)(128)(4,1)}), s8[4194304]{0:T(1024)(128)(4,1)S(1)}, s32[]{:S(2)}) async-start(s8[12582912]{0:T(1024)(128)(4,1)} %bitcast.75), calls=%async_computation.13 | async-start | bytes 8388608
  511.3 23.9 %slice-start.1 = ((s8[12582912]{0:T(1024)(128)(4,1)}), s8[4194304]{0:T(1024)(128)(4,1)S(1)}, s32[]{:S(2)}) async-start(s8[12582912]{0:T(1024)(128)(4,1)} %bitcast.75), calls=%async_computation.14 | async-start | bytes 8388608
  521.7 5.1 copy-start.27
  521.7 5.1 copy-start.29
  521.8 5.1 copy-start.31
  521.8 13.4 %slice-start.2 = ((s8[12582912]{0:T(1024)(128)(4,1)}), s8[4194304]{0:T(1024)(128)(4,1)S(1)}, s32[]{:S(2)}) async-start(s8[12582912]{0:T(1024)(128)(4,1)} %bitcast.75), calls=%async_computation.15 | async-start | bytes 8388608
  535.2 6.1 copy-start.10
  551.4 387.6 %all-reduce.6.cloned.1.call-start = ((), (), s32[]{:S(2)}) async-start(), calls=%async_computation.12 | async-start | bytes 36700160 | tf_op jit(solution)/shard_map/psum | solution.py:167
  551.4 15.6 %copy-start.38 = (bf16[2048,1024]{1,0:T(8,128)(2,1)S(1)}, bf16[2048,1024]{1,0:T(8,128)(2,1)}, u32[]{:S(2)}) copy-start(bf16[2048,1024]{1,0:T(8,128)(2,1)} %all-gather.7.cloned.1.call-done) | copy-start | bytes 12582916
  551.5 29.7 %slice-start.7 = ((s8[9437184]{0:T(1024)(128)(4,1)}), s8[4194304]{0:T(1024)(128)(4,1)S(1)}, s32[]{:S(2)}) async-start(s8[9437184]{0:T(1024)(128)(4,1)} %bitcast.92), calls=%async_computation.20 | async-start | bytes 8388608
  551.5 29.7 %slice-start.8 = ((s8[9437184]{0:T(1024)(128)(4,1)}), s8[4194304]{0:T(1024)(128)(4,1)S(1)}, s32[]{:S(2)}) async-start(s8[9437184]{0:T(1024)(128)(4,1)} %bitcast.92), calls=%async_computation.21 | async-start | bytes 8388608
  567.1 14.1 %slice-start.9 = ((s8[9437184]{0:T(1024)(128)(4,1)}), s8[1048576]{0:T(1024)(128)(4,1)S(1)}, s32[]{:S(2)}) async-start(s8[9437184]{0:T(1024)(128)(4,1)} %bitcast.92), calls=%async_computation.22 | async-start | bytes 2097152
  581.2 12.4 %copy-start.9 = (bf16[2048,1024]{1,0:T(8,128)(2,1)S(1)}, bf16[2048,1024]{1,0:T(8,128)(2,1)}, u32[]{:S(2)}) copy-start(bf16[2048,1024]{1,0:T(8,128)(2,1)} %all-gather.11.cloned.1.call-done) | copy-start | bytes 12582916
  581.2 12.4 %copy-start.13 = (bf16[2048,512]{1,0:T(8,128)(2,1)S(1)}, bf16[2048,512]{1,0:T(8,128)(2,1)}, u32[]{:S(2)}) copy-start(bf16[2048,512]{1,0:T(8,128)(2,1)} %copy-done.12) | copy-start | bytes 6291460
  593.6 4.5 copy-start.36
  606.7 41.0 %copy-start.18 = (f32[1024]{0:T(1024)S(1)}, f32[1024]{0:T(1024)}, u32[]{:S(2)}) copy-start(f32[1024]{0:T(1024)} %copy-done.17) | copy-start | bytes 12292
  606.7 41.0 %copy-start.23 = (f32[1024]{0:T(1024)S(1)}, f32[1024]{0:T(1024)}, u32[]{:S(2)}) copy-start(f32[1024]{0:T(1024)} %param.12) | copy-start | bytes 12292
  612.2 77.3 %copy-start.32 = (f32[1024]{0:T(1024)S(1)}, f32[1024]{0:T(1024)}, u32[]{:S(2)}) copy-start(f32[1024]{0:T(1024)} %get-tuple-element.32) | copy-start | bytes 12292
  942.0 4.1 copy-start.8
  942.0 9.6 slice-start.5
  946.1 5.5 slice-start.6
  946.1 10.0 %slice-start.3 = ((s8[4718592]{0:T(1024)(128)(4,1)}), s8[4194304]{0:T(1024)(128)(4,1)S(1)}, s32[]{:S(2)}) async-start(s8[4718592]{0:T(1024)(128)(4,1)} %bitcast.80), calls=%async_computation.16 | async-start | bytes 8388608
  951.6 4.5 slice-start.4
  (11 other events, 24.5 us)
Sparse Core Ops, SparseCore 0:
  14.2 59.4 all-gather.4
  96.7 54.2 reduce-scatter.4
  156.9 56.7 all-gather.6
  215.8 56.7 all-gather.8
  336.7 54.3 reduce-scatter.8
  393.2 54.3 reduce-scatter.6
  454.5 56.7 all-gather.10
  551.5 54.3 reduce-scatter.10
  612.1 326.8 all-reduce.5
where the time goes:
time: 976 us; the launch traced here: 968 us
  waiting for transfers between devices  582 us (60%)
  matrix products  200 us (20%)
  other arithmetic  84.3 us (9%)
  blocking collectives  73.3 us (8%)
  between operations  14.6 us (1%)
  local copies, waits for them, and re-layouts  13.3 us (1%)
    psum x1, waiting for transfers between devices, local(): lax.psum(in_weight_grad.astype(jnp.bfloat16), 'dp').astype(jnp.float32)  245 us
    all_gather x1, waiting for transfers between devices, local(): lax.all_gather(hidden_grad.astype(jnp.bfloat16), 'tensor', axis=0, tiled=...  56.8 us
    all_gather x1, waiting for transfers between devices, local(): lax.all_gather(normed_one.astype(jnp.bfloat16), 'tensor', axis=0, tiled=T...  54.9 us
    reduce_scatter x1, waiting for transfers between devices, local(): lax.psum_scatter(jnp.dot(gated, out_weight, preferred_element_type=jnp.fl...  54.4 us
    reduce_scatter x1, waiting for transfers between devices, local(): lax.psum_scatter(jnp.dot(inner_low, down_weight, preferred_element_type=j...  52.6 us
    all_gather x1, waiting for transfers between devices, local(): lax.all_gather(normed_two.astype(jnp.bfloat16), 'tensor', axis=0, tiled=T...  52.2 us
    reduce_scatter x1, waiting for transfers between devices, local(): lax.psum_scatter((from_gate + jnp.einsum('rf,df->rd', up_grad, up_weight,...  39.1 us
    psum x1, blocking collectives, local(): lax.psum((mixer_gain_part, ffn_gain_part), ('dp', 'tensor'))  38.5 us
  transfers between devices with their start and end apart: 9, of which 8 were waited for; matrix products, arithmetic and copies ran while one was open for 13% of the time, Pallas kernels for 0%

commit v1 on v0

--- a/solution.py
+++ b/solution.py
@@ -1,3 +1,4 @@
+import functools
 import jax
 import jax.numpy as jnp
 from jax import lax
@@ -5,6 +6,14 @@
 
 KERNEL = 3
 eps = 1e-05
+
+
+def files_produce(mine, ax_name):
+    val2 = lax.all_gather(mine, ax_name)
+    return jnp.sum(val2, 0)
+
+
+wait_ladders = functools.partial(files_produce, ax_name="dp")
 
 
 def rms_forward(values, gain_values):
@@ -164,7 +173,7 @@
         up_weight_grad,
         down_weight_grad,
     ) = (
-        lax.psum(in_weight_grad.astype(jnp.bfloat16), "dp").astype(jnp.float32),
+        wait_ladders(in_weight_grad.astype(jnp.bfloat16)).astype(jnp.float32),
         lax.psum(conv_kernel_grad.astype(jnp.bfloat16), "dp").astype(jnp.float32),
         lax.psum(out_weight_grad.astype(jnp.bfloat16), "dp").astype(jnp.float32),
         lax.psum(gate_weight_grad.astype(jnp.bfloat16), "dp").astype(jnp.float32),

time: 976 us -> 1150 us (1.18)
  waiting for transfers between devices: 582 us -> 714 us
  other arithmetic: 84.3 us -> 118 us
    all_gather x0 -> x1, waiting for transfers between devices: none -> 201 us  [files_produce(): val2 = lax.all_gather(mine, ax_name)]
    psum x1, waiting for transfers between devices: 245 us -> 181 us  [local(): lax.psum(out_weight_grad.astype(jnp.bfloat16), 'dp').astype(jnp.float32)]
    all_gather x1, waiting for transfers between devices: 56.8 us -> 14.8 us  [local(): lax.all_gather(hidden_grad.astype(jnp.bfloat16), 'tensor', axis=0, tiled=...]
    reduce_scatter x1, waiting for transfers between devices: 0.01 us -> 37.1 us  [local(): lax.psum_scatter(jnp.einsum('rkc,dkc->rd', projected_grad, in_weight, pre...]
    reduce_sum x0 -> x1, other arithmetic: none -> 18.3 us  [files_produce(): return jnp.sum(val2, 0)]
  transfers between devices with their start and end apart: 9 -> 10, of which waited for: 8 -> 10; matrix products, arithmetic and copies ran while one was open for 13% -> 17% of each run, Pallas kernels for 0% -> 0%
where the time goes in v1:
time: 1150 us; the launch traced here: 1140 us
  waiting for transfers between devices  714 us (62%)
  matrix products  209 us (18%)
  other arithmetic  118 us (10%)
  blocking collectives  75.5 us (7%)
  between operations  15 us (1%)
    all_gather x1, waiting for transfers between devices, files_produce(): val2 = lax.all_gather(mine, ax_name)  201 us
    psum x1, waiting for transfers between devices, local(): lax.psum(out_weight_grad.astype(jnp.bfloat16), 'dp').astype(jnp.float32)  181 us
    all_gather x1, waiting for transfers between devices, local(): lax.all_gather(normed_one.astype(jnp.bfloat16), 'tensor', axis=0, tiled=T...  54.9 us
    reduce_scatter x1, waiting for transfers between devices, local(): lax.psum_scatter(jnp.dot(gated, out_weight, preferred_element_type=jnp.fl...  54.2 us
    all_gather x1, waiting for transfers between devices, local(): lax.all_gather(normed_two.astype(jnp.bfloat16), 'tensor', axis=0, tiled=T...  53.3 us
    reduce_scatter x1, waiting for transfers between devices, local(): lax.psum_scatter(jnp.dot(inner_low, down_weight, preferred_element_type=j...  52.5 us
    psum x1, blocking collectives, local(): lax.psum((mixer_gain_part, ffn_gain_part), ('dp', 'tensor'))  40.7 us
    reduce_scatter x1, waiting for transfers between devices, local(): lax.psum_scatter((from_gate + jnp.einsum('rf,df->rd', up_grad, up_weight,...  38.7 us
  transfers between devices with their start and end apart: 10, of which 10 were waited for; matrix products, arithmetic and copies ran while one was open for 17% of the time, Pallas kernels for 0%

profile of v1, /device:TPU:0, one launch (start us, length us, event | category | flops | bytes accessed | tf_op | source)
XLA Modules:
  0.0 1139.1 jit_solution(5501214581542693112)
XLA Ops:
  7.2 2.1 fusion.12
  10.0 3.5 fusion.14
  13.5 4.6 copy.24
  18.2 54.9 %all-gather.7.cloned.1.call-done = bf16[2048,1024]{1,0:T(8,128)(2,1)} async-done(((bf16[1024,1024]{1,0:T(8,128)(2,1)}), bf16[2048,1024]{1,0:T(8,128)(2,1)}) %all-gather.7.cloned.1.call-update) | async-done | bytes 4194320 | tf_op jit(solution)/shard_map/all_gather | solution.py:52
  73.1 9.5 fusion.26
  82.5 3.5 slice_multiply_fusion
  86.0 8.4 multiply_add_fusion.1
  97.7 4.4 convolution_convert_fusion.4
  102.4 54.2 %reduce-scatter.5.cloned.1.call-done = bf16[1024,1024]{1,0:T(8,128)(2,1)} async-done(((bf16[2048,1024]{1,0:T(8,128)(2,1)}), bf16[1024,1024]{1,0:T(8,128)(2,1)}) %reduce-scatter.5.cloned.1.call-update) | async-done | bytes 2097168 | tf_op jit(solution)/shard_map/reduce_scatter | solution.py:70
  156.6 2.5 multiply_reduce_fusion.2
  162.6 3.3 fusion.28
  166.0 53.3 %all-gather.9.cloned.1.call-done = bf16[2048,1024]{1,0:T(8,128)(2,1)} async-done(((bf16[1024,1024]{1,0:T(8,128)(2,1)}), bf16[2048,1024]{1,0:T(8,128)(2,1)}) %all-gather.9.cloned.1.call-update) | async-done | bytes 4194320 | tf_op jit(solution)/shard_map/all_gather | solution.py:77
  219.3 16.9 %fusion.46 = f32[2048,2304]{1,0:T(8,128)} fusion(bf16[2048,1024]{1,0:T(8,128)(2,1)} %all-gather.9.cloned.1.call-done, bf16[1024,2304]{1,0:T(8,128)(2,1)} %param.18), kind=kOutput, calls=%fused_computation.96 | convolution fusion | flops 9663676416 | bytes 27787264 | tf_op jit(solution)/shard_map/dot_general | solution.py:79
  236.1 15.3 %fusion.45 = f32[2048,2304]{1,0:T(8,128)} fusion(bf16[2048,1024]{1,0:T(8,128)(2,1)S(1)} %copy-done.27, bf16[1024,2304]{1,0:T(8,128)(2,1)} %param.17), kind=kOutput, calls=%fused_computation.95 | convolution fusion | flops 9663676416 | bytes 27787264 | tf_op jit(solution)/shard_map/dot_general | solution.py:78
  251.4 26.7 %all-gather.11.cloned.1.call-done = bf16[2048,1024]{1,0:T(8,128)(2,1)} async-done(((bf16[1024,1024]{1,0:T(8,128)(2,1)}), bf16[2048,1024]{1,0:T(8,128)(2,1)}) %all-gather.11.cloned.1.call-update) | async-done | bytes 4194320 | tf_op jit(solution)/shard_map/all_gather | solution.py:102
  278.1 35.6 %multiply_convert_fusion = (bf16[2048,2304]{1,0:T(8,128)(2,1)}, bf16[2048,2304]{1,0:T(8,128)(2,1)}, bf16[2048,2304]{1,0:T(8,128)(2,1)}) fusion(f32[2048,2304]{1,0:T(8,128)} %fusion.45, f32[2048,2304]{1,0:T(8,128)} %fusion.46, bf16[2048,1024]{1,0:T(8,128)(2,1)} %all-gather.11.cloned.1.call-done, bf16[2304,1024]{1,0:T(8,128)(2,1)} %param.19), kind=kOutput, calls=%fused_computation | convolution fusion | flops 9734455296 | bytes 74973184 | tf_op jit(solution)/shard_map/rd,fd->rf/dot_general | solution.py:103
  313.7 16.1 %fusion.47 = f32[2048,1024]{1,0:T(8,128)} fusion(bf16[2048,2304]{1,0:T(8,128)(2,1)} %get-tuple-element.26, bf16[1024,2304]{1,0:T(8,128)(2,1)} %param.17), kind=kOutput, calls=%fused_computation.97 | convolution fusion | flops 9663676416 | bytes 22544384 | tf_op jit(solution)/shard_map/rf,df->rd/dot_general | solution.py:117
  329.8 14.6 %add_convert_fusion = bf16[2048,1024]{1,0:T(8,128)(2,1)} fusion(f32[2048,1024]{1,0:T(8,128)} %fusion.47, bf16[2048,2304]{1,0:T(8,128)(2,1)S(1)} %copy-done.29, bf16[1024,2304]{1,0:T(8,128)(2,1)} %param.18), kind=kOutput, calls=%fused_computation.12 | convolution fusion | flops 9667870720 | bytes 26738688 | tf_op jit(solution)/shard_map/rf,df->rd/dot_general | solution.py:121
  344.4 15.7 %convolution_convert_fusion.3 = bf16[2048,1024]{1,0:T(8,128)(2,1)} fusion(bf16[2048,2304]{1,0:T(8,128)(2,1)} %get-tuple-element.27, bf16[2304,1024]{1,0:T(8,128)(2,1)} %param.19), kind=kOutput, calls=%fused_computation.66 | convolution fusion | flops 9665773568 | bytes 18350080 | tf_op jit(solution)/shard_map/dot_general | solution.py:86
  360.2 38.7 %reduce-scatter.9.cloned.1.call-done = bf16[1024,1024]{1,0:T(8,128)(2,1)} async-done(((bf16[2048,1024]{1,0:T(8,128)(2,1)}), bf16[1024,1024]{1,0:T(8,128)(2,1)}) %reduce-scatter.9.cloned.1.call-update) | async-done | bytes 2097168 | tf_op jit(solution)/shard_map/reduce_scatter | solution.py:118
  398.9 3.9 fusion.11
  402.8 52.5 %reduce-scatter.7.cloned.1.call-done = bf16[1024,1024]{1,0:T(8,128)(2,1)} async-done(((bf16[2048,1024]{1,0:T(8,128)(2,1)}), bf16[1024,1024]{1,0:T(8,128)(2,1)}) %reduce-scatter.7.cloned.1.call-update) | async-done | bytes 2097168 | tf_op jit(solution)/shard_map/reduce_scatter | solution.py:85
  455.3 6.8 fusion.42
  462.2 15.6 %convolution_convert_fusion.2 = bf16[2304,1024]{1,0:T(8,128)(2,1)} fusion(bf16[2048,2304]{1,0:T(8,128)(2,1)} %get-tuple-element.27, bf16[2048,1024]{1,0:T(8,128)(2,1)} %all-gather.11.cloned.1.call-done), kind=kOutput, calls=%fused_computation.16 | convolution fusion | flops 9666035712 | bytes 18350080 | tf_op jit(solution)/shard_map/rf,rd->fd/dot_general | solution.py:104
  477.8 14.1 %convolution_convert_fusion = bf16[1024,2304]{1,0:T(8,128)(2,1)} fusion(bf16[2048,1024]{1,0:T(8,128)(2,1)S(1)} %copy-done.28, bf16[2048,2304]{1,0:T(8,128)(2,1)} %get-tuple-element.25), kind=kOutput, calls=%fused_computation.14 | convolution fusion | flops 9666035712 | bytes 18350080 | tf_op jit(solution)/shard_map/rd,rf->df/dot_general | solution.py:114
  491.9 12.3 %convolution_convert_fusion.1 = bf16[1024,2304]{1,0:T(8,128)(2,1)} fusion(bf16[2048,1024]{1,0:T(8,128)(2,1)S(1)} %copy-done.28, bf16[2048,2304]{1,0:T(8,128)(2,1)S(1)} %bitcast.95), kind=kOutput, calls=%fused_computation.15 | convolution fusion | flops 9666035712 | bytes 18350080 | tf_op jit(solution)/shard_map/rd,rf->df/dot_general | solution.py:111
  504.2 14.8 %all-gather.13.cloned.1.call-done = bf16[2048,1024]{1,0:T(8,128)(2,1)} async-done(((bf16[1024,1024]{1,0:T(8,128)(2,1)}), bf16[2048,1024]{1,0:T(8,128)(2,1)}) %all-gather.13.cloned.1.call-update) | async-done | bytes 4194320 | tf_op jit(solution)/shard_map/all_gather | solution.py:129
  519.0 6.2 convolution_convert_fusion.5
  525.4 10.3 multiply_reduce_fusion.1
  535.7 9.3 multiply_add_fusion
  545.0 5.6 fusion.23
  550.7 6.2 fusion.20
  556.9 10.1 bitcast_convert_fusion
  567.1 12.1 %fusion.31 = bf16[1024,3,512]{2,0,1:T(8,128)(2,1)} fusion(bf16[2048,1,512]{2,0,1:T(8,128)(2,1)} %get-tuple-element.29, bf16[2048,1,512]{2,0,1:T(8,128)(2,1)} %bitcast.87, bf16[2048,1,512]{2,0,1:T(8,128)(2,1)} %get-tuple-element.28, bf16[2048,1024]{1,0:T(8,128)(2,1)} %all-gather.7.cloned.1.call-done), kind=kOutput, calls=%fused_computation.69 | convolution fusion | flops 6462898176 | bytes 13631488 | tf_op jit(solution)/shard_map/rd,rkc->dkc/dot_general | solution.py:155
  579.3 6.2 fusion.19
  585.5 34.8 %psum.50 = bf16[3,512]{1,0:T(4,128)(2,1)S(1)} all-reduce(bf16[3,512]{1,0:T(4,128)(2,1)S(1)} %pad_maximum_fusion.5), channel_id=1, replica_groups=mesh['dp'=16,'tensor'=2] {'dp'}, use_global_device_ids=true, to_apply=%region_15.16 | all-reduce | flops 1536 | bytes 6144 | tf_op jit(solution)/shard_map/psum | solution.py:177
  620.9 181.1 %all-reduce.6.cloned.1.call-done = (bf16[512,1024]{1,0:T(8,128)(2,1)}, bf16[1024,2304]{1,0:T(8,128)(2,1)}, bf16[1024,2304]{1,0:T(8,128)(2,1)}, bf16[2304,1024]{1,0:T(8,128)(2,1)}) async-done(((bf16[512,1024]{1,0:T(8,128)(2,1)}, bf16[1024,2304]{1,0:T(8,128)(2,1)}, bf16[1024,2304]{1,0:T(8,128)(2,1)}, bf16[2304,1024]{1,0:T(8,128)(2,1)}), (bf16[512,1024]{1,0:T(8,128)(2,1)}, bf16[1024,2304]{1,0:T(8,128)(2,1)}, ...) | async-done | bytes 15204368 | tf_op jit(solution)/shard_map/psum | solution.py:178
  802.0 2.9 convert_element_type.137
  804.9 7.0 convert_element_type.139
  812.0 4.4 convert_element_type.141
  816.4 4.9 convert_element_type.143
  821.3 37.1 %reduce-scatter.11.cloned.1.call-done = bf16[1024,1024]{1,0:T(8,128)(2,1)} async-done(((bf16[2048,1024]{1,0:T(8,128)(2,1)}), bf16[1024,1024]{1,0:T(8,128)(2,1)}) %reduce-scatter.11.cloned.1.call-update) | async-done | bytes 2097168 | tf_op jit(solution)/shard_map/reduce_scatter | solution.py:158
  858.5 3.2 fusion.18
  861.7 40.7 %all-reduce.2 = (f32[1024]{0:T(1024)}, f32[1024]{0:T(1024)}) all-reduce(f32[1024]{0:T(1024)S(1)} %get-tuple-element.14, f32[1024]{0:T(1024)S(1)} %get-tuple-element.12), channel_id=1, replica_groups=mesh['dp'=16,'tensor'=2] {'dp','tensor'}, use_global_device_ids=true, to_apply=%region_10.11 | all-reduce | flops 2048 | bytes 16384 | tf_op jit(solution)/shard_map/psum | solution.py:183
  902.4 4.7 fusion.6
  907.1 200.9 %all-gather.15.cloned.1.call-done = bf16[16384,3,512]{2,0,1:T(8,128)(2,1)} async-done(((bf16[1024,3,512]{2,0,1:T(8,128)(2,1)}), bf16[16384,3,512]{2,0,1:T(8,128)(2,1)}) %all-gather.15.cloned.1.call-update) | async-done | bytes 50331664 | tf_op jit(solution)/shard_map/all_gather | solution.py:12
  1108.0 18.3 %reduce_sum.98 = bf16[1024,3,512]{2,0,1:T(8,128)(2,1)} reduce(bf16[16,1024,3,512]{3,1,0,2:T(8,128)(2,1)} %bitcast.78, bf16[]{:T(256)} %constant.49.clone.1), dimensions={0}, to_apply=%region_11.12 | reduce | flops 23592960 | bytes 53477376 | tf_op jit(solution)/shard_map/reduce_sum | solution.py:13
  1126.4 5.5 convert_element_type.134
  (119 shorter events, 8.9 us)
Async XLA Ops:
  7.2 90.6 %copy-start = (bf16[512,1024]{1,0:T(8,128)(2,1)S(1)}, bf16[512,1024]{1,0:T(8,128)(2,1)}, u32[]{:S(2)}) copy-start(bf16[512,1024]{1,0:T(8,128)(2,1)} %param.15) | copy-start | bytes 3145732
  7.2 65.9 %all-gather.7.cloned.1.call-start = ((), (), s32[]{:S(2)}) async-start(), calls=%async_computation.4 | async-start | bytes 6291456 | tf_op jit(solution)/shard_map/all_gather | solution.py:52
  10.0 8.2 copy-start.8
  13.5 4.7 copy-start.25
  13.5 143.1 %reduce-scatter.5.cloned.1.call-start = ((), (), s32[]{:S(2)}) async-start(), calls=%async_computation.5 | async-start | bytes 6291456 | tf_op jit(solution)/shard_map/reduce_scatter | solution.py:70
  18.2 67.8 %copy-start.17 = (f32[1,512]{1,0:T(1,128)}, f32[1,512]{1,0:T(1,128)S(1)}, u32[]{:S(2)}) copy-start(f32[1,512]{1,0:T(1,128)S(1)} %get-tuple-element.35) | copy-start | bytes 6148
  18.2 67.8 %copy-start.19 = (f32[1,512]{1,0:T(1,128)}, f32[1,512]{1,0:T(1,128)S(1)}, u32[]{:S(2)}) copy-start(f32[1,512]{1,0:T(1,128)S(1)} %get-tuple-element.36) | copy-start | bytes 6148
  18.2 67.8 %copy-start.21 = (f32[1,512]{1,0:T(1,128)}, f32[1,512]{1,0:T(1,128)S(1)}, u32[]{:S(2)}) copy-start(f32[1,512]{1,0:T(1,128)S(1)} %get-tuple-element.37) | copy-start | bytes 6148
  82.5 11.9 %copy-start.3 = (f32[2048,3,512]{2,0,1:T(8,128)}, f32[2048,3,512]{2,0,1:T(8,128)S(1)}, u32[]{:S(2)}) copy-start(f32[2048,3,512]{2,0,1:T(8,128)S(1)} %fusion.26) | copy-start | bytes 37748740
  94.4 2.0 copy-start.4
  102.1 54.5 %copy-start.1 = (bf16[1024,1024]{1,0:T(8,128)(2,1)S(1)}, bf16[1024,1024]{1,0:T(8,128)(2,1)}, u32[]{:S(2)}) copy-start(bf16[1024,1024]{1,0:T(8,128)(2,1)} %param.11) | copy-start | bytes 6291460
  102.1 58.2 %copy-start.12 = (f32[1024]{0:T(1024)S(1)}, f32[1024]{0:T(1024)}, u32[]{:S(2)}) copy-start(f32[1024]{0:T(1024)} %param.16) | copy-start | bytes 12292
  102.1 117.2 %all-gather.9.cloned.1.call-start = ((), (), s32[]{:S(2)}) async-start(), calls=%async_computation.6 | async-start | bytes 6291456 | tf_op jit(solution)/shard_map/all_gather | solution.py:77
  156.6 3.7 copy-start.5
  160.3 2.2 copy-start.26
  162.4 115.7 %all-gather.11.cloned.1.call-start = ((), (), s32[]{:S(2)}) async-start(), calls=%async_computation.8 | async-start | bytes 6291456 | tf_op jit(solution)/shard_map/all_gather | solution.py:102
  162.6 73.6 %copy-start.15 = (f32[1024]{0:T(1024)}, f32[1024]{0:T(1024)S(1)}, u32[]{:S(2)}) copy-start(f32[1024]{0:T(1024)S(1)} %convert_element_type.123) | copy-start | bytes 12292
  165.9 232.9 %reduce-scatter.9.cloned.1.call-start = ((), (), s32[]{:S(2)}) async-start(), calls=%async_computation.9 | async-start | bytes 6291456 | tf_op jit(solution)/shard_map/reduce_scatter | solution.py:118
  219.3 16.9 %copy-start.27 = (bf16[2048,1024]{1,0:T(8,128)(2,1)S(1)}, bf16[2048,1024]{1,0:T(8,128)(2,1)}, u32[]{:S(2)}) copy-start(bf16[2048,1024]{1,0:T(8,128)(2,1)} %all-gather.9.cloned.1.call-done) | copy-start | bytes 12582916
  313.7 16.1 %copy-start.29 = (bf16[2048,2304]{1,0:T(8,128)(2,1)S(1)}, bf16[2048,2304]{1,0:T(8,128)(2,1)}, u32[]{:S(2)}) copy-start(bf16[2048,2304]{1,0:T(8,128)(2,1)} %get-tuple-element.25) | copy-start | bytes 28311556
  344.4 110.9 %reduce-scatter.7.cloned.1.call-start = ((), (), s32[]{:S(2)}) async-start(), calls=%async_computation.7 | async-start | bytes 6291456 | tf_op jit(solution)/shard_map/reduce_scatter | solution.py:85
  360.1 38.8 %copy-start.2 = (bf16[1024,1024]{1,0:T(8,128)(2,1)S(1)}, bf16[1024,1024]{1,0:T(8,128)(2,1)}, u32[]{:S(2)}) copy-start(bf16[1024,1024]{1,0:T(8,128)(2,1)} %param.11) | copy-start | bytes 6291460
  360.1 38.8 %copy-start.11 = (f32[1024]{0:T(1024)S(1)}, f32[1024]{0:T(1024)}, u32[]{:S(2)}) copy-start(f32[1024]{0:T(1024)} %copy-done.10) | copy-start | bytes 12292
  360.1 38.8 %copy-start.13 = (f32[1024]{0:T(1024)S(1)}, f32[1024]{0:T(1024)}, u32[]{:S(2)}) copy-start(f32[1024]{0:T(1024)} %param.16) | copy-start | bytes 12292
  360.1 95.2 %copy-start.16 = (f32[1024]{0:T(1024)S(1)}, f32[1024]{0:T(1024)}, u32[]{:S(2)}) copy-start(f32[1024]{0:T(1024)} %copy-done.15) | copy-start | bytes 12292
  360.1 95.2 %copy-start.24 = (f32[1024]{0:T(1024)S(1)}, f32[1024]{0:T(1024)}, u32[]{:S(2)}) copy-start(f32[1024]{0:T(1024)} %get-tuple-element.33) | copy-start | bytes 12292
  360.1 158.9 %all-gather.13.cloned.1.call-start = ((), (), s32[]{:S(2)}) async-start(), calls=%async_computation.10 | async-start | bytes 6291456 | tf_op jit(solution)/shard_map/all_gather | solution.py:129
  462.1 339.9 %all-reduce.6.cloned.1.call-start = ((), (), s32[]{:S(2)}) async-start(), calls=%async_computation.13 | async-start | bytes 30408704 | tf_op jit(solution)/shard_map/psum | solution.py:178
  462.2 15.6 %copy-start.28 = (bf16[2048,1024]{1,0:T(8,128)(2,1)S(1)}, bf16[2048,1024]{1,0:T(8,128)(2,1)}, u32[]{:S(2)}) copy-start(bf16[2048,1024]{1,0:T(8,128)(2,1)} %all-gather.9.cloned.1.call-done) | copy-start | bytes 12582916
  462.2 29.7 %slice-start.7 = ((s8[9437184]{0:T(1024)(128)(4,1)}), s8[4194304]{0:T(1024)(128)(4,1)S(1)}, s32[]{:S(2)}) async-start(s8[9437184]{0:T(1024)(128)(4,1)} %bitcast.94), calls=%async_computation.21 | async-start | bytes 8388608
  462.2 29.7 %slice-start.8 = ((s8[9437184]{0:T(1024)(128)(4,1)}), s8[4194304]{0:T(1024)(128)(4,1)S(1)}, s32[]{:S(2)}) async-start(s8[9437184]{0:T(1024)(128)(4,1)} %bitcast.94), calls=%async_computation.22 | async-start | bytes 8388608
  477.8 14.1 %slice-start.9 = ((s8[9437184]{0:T(1024)(128)(4,1)}), s8[1048576]{0:T(1024)(128)(4,1)S(1)}, s32[]{:S(2)}) async-start(s8[9437184]{0:T(1024)(128)(4,1)} %bitcast.94), calls=%async_computation.23 | async-start | bytes 2097152
  525.3 10.4 copy-start.18
  525.3 10.4 copy-start.20
  525.3 10.4 copy-start.22
  525.3 333.2 %reduce-scatter.11.cloned.1.call-start = ((), (), s32[]{:S(2)}) async-start(), calls=%async_computation.11 | async-start | bytes 6291456 | tf_op jit(solution)/shard_map/reduce_scatter | solution.py:158
  525.3 25.3 %slice-start = ((s8[12582912]{0:T(1024)(128)(4,1)}), s8[4194304]{0:T(1024)(128)(4,1)S(1)}, s32[]{:S(2)}) async-start(s8[12582912]{0:T(1024)(128)(4,1)} %bitcast.76), calls=%async_computation.14 | async-start | bytes 8388608
  525.4 25.3 %slice-start.1 = ((s8[12582912]{0:T(1024)(128)(4,1)}), s8[4194304]{0:T(1024)(128)(4,1)S(1)}, s32[]{:S(2)}) async-start(s8[12582912]{0:T(1024)(128)(4,1)} %bitcast.76), calls=%async_computation.15 | async-start | bytes 8388608
  535.7 15.0 %slice-start.2 = ((s8[12582912]{0:T(1024)(128)(4,1)}), s8[4194304]{0:T(1024)(128)(4,1)S(1)}, s32[]{:S(2)}) async-start(s8[12582912]{0:T(1024)(128)(4,1)} %bitcast.76), calls=%async_computation.16 | async-start | bytes 8388608
  550.7 6.2 copy-start.6
  567.0 541.0 %all-gather.15.cloned.1.call-start = ((), (), s32[]{:S(2)}) async-start(), calls=%async_computation.12 | async-start | bytes 53477376 | tf_op jit(solution)/shard_map/all_gather | solution.py:12
  802.0 10.0 slice-start.5
  804.9 7.0 slice-start.6
  804.9 11.5 %slice-start.3 = ((s8[4718592]{0:T(1024)(128)(4,1)}), s8[4194304]{0:T(1024)(128)(4,1)S(1)}, s32[]{:S(2)}) async-start(s8[4718592]{0:T(1024)(128)(4,1)} %bitcast.82), calls=%async_computation.17 | async-start | bytes 8388608
  811.9 4.5 slice-start.4
  816.4 42.0 %copy-start.9 = (f32[1024]{0:T(1024)S(1)}, f32[1024]{0:T(1024)}, u32[]{:S(2)}) copy-start(f32[1024]{0:T(1024)} %copy-done.8) | copy-start | bytes 12292
  816.4 42.0 %copy-start.14 = (f32[1024]{0:T(1024)S(1)}, f32[1024]{0:T(1024)}, u32[]{:S(2)}) copy-start(f32[1024]{0:T(1024)} %param.12) | copy-start | bytes 12292
  821.3 81.0 %copy-start.23 = (f32[1024]{0:T(1024)S(1)}, f32[1024]{0:T(1024)}, u32[]{:S(2)}) copy-start(f32[1024]{0:T(1024)} %get-tuple-element.31) | copy-start | bytes 12292
  (2 other events, 1.9 us)
Sparse Core Ops, SparseCore 0:
  13.6 59.4 all-gather.6
  102.2 54.2 reduce-scatter.4
  162.5 56.7 all-gather.8
  221.3 56.7 all-gather.10
  344.5 54.3 reduce-scatter.8
  401.0 54.2 reduce-scatter.6
  462.2 56.7 all-gather.12
  525.4 276.5 all-reduce.5
  804.4 54.0 reduce-scatter.10
  859.8 248.1 all-gather.14
